TPU v7x, 32 devices: a whole 2x2x4 slice. The times are simulated.
32 devices in a mesh: dp: 8 (over z, y), seq: 4 (over x, core).
Axes of the slice: x: 2, y: 2, z: 4, core: 2. Of those that a mesh axis runs over, the one named last changes fastest.
Arguments:
- hidden_in: bfloat16 [32, 1024, 768], P('dp', 'seq'), may hold values from -6 to 6
- time_table: bfloat16 [1024, 128], replicated, may hold values from -6 to 6
- time_step: int32 [32], P('dp'), may hold values from 0 to 1023
- token_pos: int32 [32, 1024], P('dp', 'seq'), may hold values from 0 to 3071, as said below
- heads_weight: bfloat16 [768, 2304], P('seq'), may hold values from -0.15625 to 0.15625
- merge_weight: bfloat16 [768, 768], P('seq'), may hold values from -1.75 to 1.75
- lift_weight: bfloat16 [768, 3072], P('seq'), may hold values from -0.21875 to 0.21875
- lift_bias: bfloat16 [3072], P('seq'), may hold values from -3 to 3
- drop_weight: bfloat16 [3072, 768], P('seq'), may hold values from -0.109375 to 0.109375
- drop_bias: bfloat16 [768], P('seq'), may hold values from -3 to 3
- modulate_weight: bfloat16 [4608, 128], P('seq'), may hold values from -0.5 to 0.5
- modulate_bias: bfloat16 [4608], P('seq'), may hold values from -3 to 3
- first_gain: bfloat16 [768], P('seq'), may hold values from 0.099609375 to 1.8984375
- second_gain: bfloat16 [768], P('seq'), may hold values from 0.099609375 to 1.8984375
- out_grad: bfloat16 [32, 1024, 768], P('dp', 'seq'), may hold values from -6 to 6
Outputs:
- block_out: bfloat16 [32, 1024, 768], P('dp', 'seq')
- input_grad: bfloat16 [32, 1024, 768], P('dp', 'seq')
- heads_grad: float32 [768, 2304], P('seq')
- merge_grad: float32 [768, 768], P('seq')
- lift_grad: float32 [768, 3072], P('seq')
- liftbias_grad: float32 [3072], P('seq')
- drop_grad: float32 [3072, 768], P('seq')
- dropbias_grad: float32 [768], P('seq')
- modulate_grad: float32 [4608, 128], P('seq')
- modulatebias_grad: float32 [4608], P('seq')
- firstgain_grad: float32 [768], P('seq')
- secondgain_grad: float32 [768], P('seq')
- table_grad: float32 [1024, 128], P('seq')
Inputs may be any that keep to these rules, and one draw needn't show every extreme that they name: `token_pos`: positions count up by one along a row and start again at 0 at each separator token; in every aligned group of 4 rows one row holds no separator; such a row in the first group starts at 2048, such a row in the second group starts at 0.
All inputs are finite; a program needn't handle non-finite values.
Results may differ from a plain program's by a relative error of at most 0.017.
The roundings to bfloat16 on the way count: a program that leaves them out, or rounds other values in their place, can miss the bound.
Values may be sent and summed in bfloat16 or wider, within the bound.
No kernel may reach another device: no remote copies, remote signals or barrier semaphores. Data moves between devices by JAX's collectives and lax.ppermute only.
A program may use at most 320 MiB of HBM per device.

v0:
```python
from functools import partial
import math
import jax
import jax.numpy as jnp
from jax import lax
from jax.sharding import PartitionSpec as P

HEADS = 12
EPSILON = 1e-05


def rotate_half(values):
    middle = values.shape[-1] // 2
    return jnp.concatenate([-values[..., middle:], values[..., :middle]], axis=-1)


def rotate(values, cosine, sine):
    return values * cosine + rotate_half(values) * sine


def unrotate(values, cosine, sine):
    return values * cosine - rotate_half(values * sine)


def norm_forward(values, gain):
    center = values - jnp.mean(values, axis=-1, keepdims=True)
    inverse = lax.rsqrt(jnp.mean(center * center, axis=-1, keepdims=True) + EPSILON)
    unit = center * inverse
    return (unit, inverse, unit * gain)


def norm_backward(normed_grad, unit, inverse, gain):
    unit_grad = normed_grad * gain
    first = jnp.mean(unit_grad, axis=-1, keepdims=True)
    second = jnp.mean(unit_grad * unit, axis=-1, keepdims=True)
    return inverse * (unit_grad - first - unit * second)


def grouping(seqs, span):
    group = 1
    while group * span < 512 and seqs % (group * 2) == 0:
        group = group * 2
    return group


def shards(
    hidden_in,
    time_table,
    time_step,
    token_pos,
    heads_weight,
    merge_weight,
    lift_weight,
    lift_bias,
    drop_weight,
    drop_bias,
    modulate_weight,
    modulate_bias,
    first_gain,
    second_gain,
    out_grad,
):
    float_type = jnp.float32
    low_type = jnp.bfloat16
    position_count = lax.axis_size("seq")
    hidden_rows, upstream_rows, places_rows = (hidden_in, out_grad, token_pos)
    seqs, span, width = hidden_rows.shape
    length = span * position_count
    head_width = width // HEADS
    scale = 1.0 / math.sqrt(head_width)
    gathered = (
        lax.all_gather(heads_weight, "seq", axis=0, tiled=True),
        lax.all_gather(merge_weight, "seq", axis=0, tiled=True),
        lax.all_gather(lift_weight, "seq", axis=0, tiled=True),
        lax.all_gather(lift_bias, "seq", axis=0, tiled=True),
        lax.all_gather(drop_weight, "seq", axis=0, tiled=True),
        lax.all_gather(drop_bias, "seq", axis=0, tiled=True),
        lax.all_gather(modulate_weight, "seq", axis=0, tiled=True),
        lax.all_gather(modulate_bias, "seq", axis=0, tiled=True),
        lax.all_gather(first_gain, "seq", axis=0, tiled=True),
        lax.all_gather(second_gain, "seq", axis=0, tiled=True),
    )
    w_heads, w_merge, w_lift, b_lift, w_drop, b_drop, w_mod, b_mod, gain_one, gain_two = gathered
    gain_one = gain_one.astype(float_type)
    gain_two = gain_two.astype(float_type)
    table_rows = time_table.shape[0]
    choose = (time_step[:, None] == jnp.arange(table_rows, dtype=jnp.int32)[None, :]).astype(
        low_type
    )
    conds = jnp.dot(choose, time_table, preferred_element_type=float_type)
    modulation = lax.dot_general(
        conds.astype(low_type), w_mod, (((1,), (1,)), ((), ())), preferred_element_type=float_type
    ) + b_mod.astype(float_type)
    pieces = [piece[:, None, :] for piece in jnp.split(modulation, 6, axis=-1)]
    shift_a, scale_a, gate_a, shift_b, scale_b, gate_b = pieces
    positions = places_rows.astype(float_type)
    freqs = 10000.0 ** (-jnp.arange(0, head_width, 2, dtype=float_type) / head_width)
    angles = positions[..., None] * freqs
    angles = jnp.concatenate([angles, angles], axis=-1)
    cosine = jnp.cos(angles)[:, :, None, :]
    sine = jnp.sin(angles)[:, :, None, :]
    head_layout = (seqs, span, HEADS, head_width)
    inputs = hidden_rows.astype(float_type)
    unit_one, inverse_one, normed_one = norm_forward(inputs, gain_one)
    adapted_one = (normed_one * (1.0 + scale_a) + shift_a).astype(low_type)
    projected = jnp.einsum("scd,de->sce", adapted_one, w_heads, preferred_element_type=float_type)
    query_raw, key_raw, value_raw = jnp.split(projected, 3, axis=-1)
    query = rotate(query_raw.reshape(head_layout), cosine, sine).astype(low_type)
    keys_local = (
        rotate(key_raw.reshape(head_layout), cosine, sine)
        .astype(low_type)
        .reshape(seqs, span, width)
    )
    values_local = value_raw.astype(low_type)
    keys_all, values_all = (
        lax.all_gather(keys_local, "seq", axis=1, tiled=True),
        lax.all_gather(values_local, "seq", axis=1, tiled=True),
    )
    group = grouping(seqs, span)
    blocks = seqs // group

    def split_groups(array):
        return array.reshape((blocks, group) + array.shape[1:])

    def attend(block):
        query_b, keys_b, values_b = block
        keys_h = keys_b.reshape(group, length, HEADS, head_width)
        values_h = values_b.reshape(group, length, HEADS, head_width)
        scores = (
            jnp.einsum("gqhd,gkhd->ghqk", query_b, keys_h, preferred_element_type=float_type)
            * scale
        )
        peak = jnp.max(scores, axis=-1, keepdims=True)
        expos = jnp.exp(scores - peak)
        totals = jnp.sum(expos, axis=-1, keepdims=True)
        probs = (expos / totals).astype(low_type)
        mixed_b = jnp.einsum("ghqk,gkhd->gqhd", probs, values_h, preferred_element_type=float_type)
        return (mixed_b, peak[..., 0] + jnp.log(totals[..., 0]))

    mixed, logsum = lax.map(
        attend, (split_groups(query), split_groups(keys_all), split_groups(values_all))
    )
    mixed_low = mixed.reshape(seqs, span, width).astype(low_type)
    branch = jnp.einsum("scd,de->sce", mixed_low, w_merge, preferred_element_type=float_type)
    middle = inputs + gate_a * branch
    unit_two, inverse_two, normed_two = norm_forward(middle, gain_two)
    adapted_two = (normed_two * (1.0 + scale_b) + shift_b).astype(low_type)
    upper = jnp.einsum(
        "scd,df->scf", adapted_two, w_lift, preferred_element_type=float_type
    ) + b_lift.astype(float_type)
    active, gelu_back = jax.vjp(partial(jax.nn.gelu, approximate=True), upper)
    active_low = active.astype(low_type)
    lowered = jnp.einsum(
        "scf,fd->scd", active_low, w_drop, preferred_element_type=float_type
    ) + b_drop.astype(float_type)
    block_out = (middle + gate_b * lowered).astype(low_type)
    upstream = upstream_rows.astype(float_type)
    gate_b_grad = jnp.sum(upstream * lowered, axis=1)
    lowered_grad = (gate_b * upstream).astype(low_type)
    drop_grad = jnp.einsum(
        "scf,scd->fd", active_low, lowered_grad, preferred_element_type=float_type
    )
    dropbias_grad = jnp.sum(lowered_grad.astype(float_type), axis=(0, 1))
    active_grad = jnp.einsum("scd,fd->scf", lowered_grad, w_drop, preferred_element_type=float_type)
    (upper_grad,) = gelu_back(active_grad)
    upper_low = upper_grad.astype(low_type)
    lift_grad = jnp.einsum("scd,scf->df", adapted_two, upper_low, preferred_element_type=float_type)
    liftbias_grad = jnp.sum(upper_low.astype(float_type), axis=(0, 1))
    adapted_two_grad = jnp.einsum(
        "scf,df->scd", upper_low, w_lift, preferred_element_type=float_type
    )
    shift_b_grad = jnp.sum(adapted_two_grad, axis=1)
    scale_b_grad = jnp.sum(adapted_two_grad * normed_two, axis=1)
    normed_two_grad = adapted_two_grad * (1.0 + scale_b)
    secondgain_grad = jnp.sum(normed_two_grad * unit_two, axis=(0, 1))
    middle_grad = upstream + norm_backward(normed_two_grad, unit_two, inverse_two, gain_two)
    gate_a_grad = jnp.sum(middle_grad * branch, axis=1)
    branch_grad = (gate_a * middle_grad).astype(low_type)
    merge_grad = jnp.einsum(
        "scd,sce->de", mixed_low, branch_grad, preferred_element_type=float_type
    )
    mixed_grad = jnp.einsum(
        "sce,de->scd", branch_grad, w_merge, preferred_element_type=float_type
    ).astype(low_type)
    keys_back, values_back = (
        lax.all_gather(keys_local, "seq", axis=1, tiled=True),
        lax.all_gather(values_local, "seq", axis=1, tiled=True),
    )

    def attend_back(block):
        query_b, keys_b, values_b, logsum_b, mixed_grad_b = block
        keys_h = keys_b.reshape(group, length, HEADS, head_width)
        values_h = values_b.reshape(group, length, HEADS, head_width)
        scores = (
            jnp.einsum("gqhd,gkhd->ghqk", query_b, keys_h, preferred_element_type=float_type)
            * scale
        )
        probs = jnp.exp(scores - logsum_b[..., None])
        probs_low = probs.astype(low_type)
        values_term = jnp.einsum(
            "ghqk,gqhd->gkhd", probs_low, mixed_grad_b, preferred_element_type=float_type
        )
        probs_grad = jnp.einsum(
            "gqhd,gkhd->ghqk", mixed_grad_b, values_h, preferred_element_type=float_type
        )
        center = jnp.sum(probs * probs_grad, axis=-1, keepdims=True)
        scores_grad = (probs * (probs_grad - center)).astype(low_type)
        query_term = (
            jnp.einsum("ghqk,gkhd->gqhd", scores_grad, keys_h, preferred_element_type=float_type)
            * scale
        )
        keys_term = (
            jnp.einsum("ghqk,gqhd->gkhd", scores_grad, query_b, preferred_element_type=float_type)
            * scale
        )
        return (
            query_term,
            keys_term.reshape(group, length, width),
            values_term.reshape(group, length, width),
        )

    mixed_grad_h = mixed_grad.reshape(head_layout)
    query_term, keys_term, values_term = lax.map(
        attend_back,
        (
            split_groups(query),
            split_groups(keys_back),
            split_groups(values_back),
            logsum,
            split_groups(mixed_grad_h),
        ),
    )
    keys_grad, values_grad = (
        lax.psum_scatter(
            keys_term.reshape(seqs, length, width).astype(jnp.bfloat16),
            "seq",
            scatter_dimension=1,
            tiled=True,
        ).astype(jnp.float32),
        lax.psum_scatter(
            values_term.reshape(seqs, length, width).astype(jnp.bfloat16),
            "seq",
            scatter_dimension=1,
            tiled=True,
        ).astype(jnp.float32),
    )
    query_grad = unrotate(query_term.reshape(head_layout), cosine, sine).reshape(seqs, span, width)
    key_grad = unrotate(keys_grad.reshape(head_layout), cosine, sine).reshape(seqs, span, width)
    projected_grad = jnp.concatenate([query_grad, key_grad, values_grad], axis=-1).astype(low_type)
    heads_grad = jnp.einsum(
        "scd,sce->de", adapted_one, projected_grad, preferred_element_type=float_type
    )
    adapted_one_grad = jnp.einsum(
        "sce,de->scd", projected_grad, w_heads, preferred_element_type=float_type
    )
    shift_a_grad = jnp.sum(adapted_one_grad, axis=1)
    scale_a_grad = jnp.sum(adapted_one_grad * normed_one, axis=1)
    normed_one_grad = adapted_one_grad * (1.0 + scale_a)
    firstgain_grad = jnp.sum(normed_one_grad * unit_one, axis=(0, 1))
    input_grad = (
        middle_grad + norm_backward(normed_one_grad, unit_one, inverse_one, gain_one)
    ).astype(low_type)
    modulation_grad = jnp.concatenate(
        [shift_a_grad, scale_a_grad, gate_a_grad, shift_b_grad, scale_b_grad, gate_b_grad], axis=-1
    )
    modulate_grad = jnp.einsum("sm,sc->mc", modulation_grad, conds, precision=lax.Precision.HIGHEST)
    modulatebias_grad = jnp.sum(modulation_grad, axis=0)
    conds_grad = jnp.einsum(
        "sm,mc->sc", modulation_grad, w_mod.astype(float_type), precision=lax.Precision.HIGHEST
    )
    table_grad = jnp.einsum(
        "sn,sc->nc", choose.astype(float_type), conds_grad, precision=lax.Precision.HIGHEST
    )
    terms = (
        heads_grad,
        merge_grad,
        lift_grad,
        liftbias_grad,
        drop_grad,
        dropbias_grad,
        modulate_grad,
        modulatebias_grad,
        firstgain_grad,
        secondgain_grad,
        table_grad,
    )
    shares = (
        lax.psum_scatter(
            terms[0].astype(jnp.bfloat16), "seq", scatter_dimension=0, tiled=True
        ).astype(jnp.float32),
        lax.psum_scatter(
            terms[1].astype(jnp.bfloat16), "seq", scatter_dimension=0, tiled=True
        ).astype(jnp.float32),
        lax.psum_scatter(
            terms[2].astype(jnp.bfloat16), "seq", scatter_dimension=0, tiled=True
        ).astype(jnp.float32),
        lax.psum_scatter(
            terms[3].astype(jnp.bfloat16), "seq", scatter_dimension=0, tiled=True
        ).astype(jnp.float32),
        lax.psum_scatter(
            terms[4].astype(jnp.bfloat16), "seq", scatter_dimension=0, tiled=True
        ).astype(jnp.float32),
        lax.psum_scatter(
            terms[5].astype(jnp.bfloat16), "seq", scatter_dimension=0, tiled=True
        ).astype(jnp.float32),
        lax.psum_scatter(
            terms[6].astype(jnp.bfloat16), "seq", scatter_dimension=0, tiled=True
        ).astype(jnp.float32),
        lax.psum_scatter(
            terms[7].astype(jnp.bfloat16), "seq", scatter_dimension=0, tiled=True
        ).astype(jnp.float32),
        lax.psum_scatter(
            terms[8].astype(jnp.bfloat16), "seq", scatter_dimension=0, tiled=True
        ).astype(jnp.float32),
        lax.psum_scatter(
            terms[9].astype(jnp.bfloat16), "seq", scatter_dimension=0, tiled=True
        ).astype(jnp.float32),
        lax.psum_scatter(
            terms[10].astype(jnp.bfloat16), "seq", scatter_dimension=0, tiled=True
        ).astype(jnp.float32),
    )
    summed = lax.psum(
        (
            shares[0],
            shares[1],
            shares[2],
            shares[3],
            shares[4],
            shares[5],
            shares[6],
            shares[7],
            shares[8],
            shares[9],
            shares[10],
        ),
        "dp",
    )
    return (
        block_out,
        input_grad,
        summed[0],
        summed[1],
        summed[2],
        summed[3],
        summed[4],
        summed[5],
        summed[6],
        summed[7],
        summed[8],
        summed[9],
        summed[10],
    )


def solution(mesh):
    return jax.shard_map(
        shards,
        mesh=mesh,
        in_specs=(
            P("dp", "seq", None),
            P(),
            P("dp"),
            P("dp", "seq"),
            P("seq", None),
            P("seq", None),
            P("seq", None),
            P("seq"),
            P("seq", None),
            P("seq"),
            P("seq", None),
            P("seq"),
            P("seq"),
            P("seq"),
            P("dp", "seq", None),
        ),
        out_specs=(
            P("dp", "seq", None),
            P("dp", "seq", None),
            P("seq", None),
            P("seq", None),
            P("seq", None),
            P("seq"),
            P("seq", None),
            P("seq"),
            P("seq", None),
            P("seq"),
            P("seq"),
            P("seq"),
            P("seq", None),
        ),
        check_vma=False,
    )
```

profile of v0, /device:TPU:0, one launch (start us, length us, event | category | flops | bytes accessed | tf_op | source)
XLA Modules:
  0.0 1162.3 jit_solution(14610913163980127939)
XLA Ops:
  33.2 29.1 %all-gather.12.cloned.1.call-done = bf16[768,2304]{1,0:T(8,128)(2,1)} async-done(((bf16[192,2304]{1,0:T(8,128)(2,1)}), bf16[768,2304]{1,0:T(8,128)(2,1)}) %all-gather.12.cloned.1.call-update) | async-done | bytes 3538960 | tf_op jit(solution)/shard_map/all_gather | solution.py:72
  130.6 37.9 %all-gather.16.cloned.1.call-done = bf16[4,1024,768]{2,1,0:T(8,128)(2,1)} async-done(((bf16[4,256,768]{2,1,0:T(8,128)(2,1)}), bf16[4,1024,768]{2,1,0:T(8,128)(2,1)}) %all-gather.16.cloned.1.call-update) | async-done | bytes 6291472 | tf_op jit(solution)/shard_map/all_gather | solution.py:116
  177.2 74.9 %while.28 = (s32[]{:T(128)}, bf16[2,2,256,12,64]{2,4,3,1,0:T(8,128)(2,1)}, f32[2,2,12,256]{3,2,1,0:T(8,128)S(1)}, bf16[2,2,1024,768]{2,3,1,0:T(8,128)(2,1)}, bf1...) while((s32[]{:T(128)}, bf16[2,2,256,12,64]{2,4,3,1,0:T(8,128)(2,1)}, ...), condition=%wide.region_5.6_spmd.clone, body=%wide.region_2.5_spmd.sunk.clone | while | flops 1667229696 | bytes 96952408 | solution.py:140
  180.9 10.2 multiply_reduce_fusion.11
  191.1 11.7 %fusion.143 = f32[2,12,256]{2,1,0:T(8,128)S(1)} fusion(f32[2,12,256,1024]{3,2,1,0:T(8,128)} %get-tuple-element.385, f32[2,12,256]{2,1,0:T(8,128)S(1)} %get-tuple-element.386), kind=kLoop, calls=%fused_computation.3.clone.1.clone | loop fusion | flops 18868224 | bytes 25214976 | tf_op jit(solution)/shard_map/while/body/eval_jaxpr/reduce_sum | solution.py:135
  202.8 11.8 %bitcast_dynamic-update-slice_fusion.9 = bf16[2,2,256,12,64]{2,4,3,1,0:T(8,128)(2,1)} fusion(bf16[2,2,256,12,64]{2,4,3,1,0:T(8,128)(2,1)} %get-tuple-element.425, s32[]{:T(128)S(6)} %copy.125, bf16[2,1024,12,64]{1,3,2,0:T(8,128)(2,1)S(1)} %bitcast.191, f32[2,12,256,1024]{3,2,1,0:T(8,128)} %get-tuple-element.385, ...), kind=kOutput, calls=%fused_computation.5.clone.1.clone | convolution fusion | flops 830472192 | bytes 29933572 | tf_op jit(solution)/shard_map/while/body/eval_jaxpr/ghqk,gkhd->gqhd/dot_general | solution.py:137
  218.3 10.3 multiply_reduce_fusion.11
  228.5 11.8 %fusion.143 = f32[2,12,256]{2,1,0:T(8,128)S(1)} fusion(f32[2,12,256,1024]{3,2,1,0:T(8,128)} %get-tuple-element.385, f32[2,12,256]{2,1,0:T(8,128)S(1)} %get-tuple-element.386), kind=kLoop, calls=%fused_computation.3.clone.1.clone | loop fusion | flops 18868224 | bytes 25214976 | tf_op jit(solution)/shard_map/while/body/eval_jaxpr/reduce_sum | solution.py:135
  240.4 11.8 %bitcast_dynamic-update-slice_fusion.9 = bf16[2,2,256,12,64]{2,4,3,1,0:T(8,128)(2,1)} fusion(bf16[2,2,256,12,64]{2,4,3,1,0:T(8,128)(2,1)} %get-tuple-element.425, s32[]{:T(128)S(6)} %copy.125, bf16[2,1024,12,64]{1,3,2,0:T(8,128)(2,1)S(1)} %bitcast.191, f32[2,12,256,1024]{3,2,1,0:T(8,128)} %get-tuple-element.385, ...), kind=kOutput, calls=%fused_computation.5.clone.1.clone | convolution fusion | flops 830472192 | bytes 29933572 | tf_op jit(solution)/shard_map/while/body/eval_jaxpr/ghqk,gkhd->gqhd/dot_general | solution.py:137
  259.5 11.3 fusion.40
  270.8 16.6 %fusion.93 = (bf16[3072]{0:T(1024)(128)(2,1)}, bf16[4,256,3072]{2,1,0:T(8,128)(2,1)}) fusion(f32[4,256,3072]{2,1,0:T(8,128)} %fusion.40, f32[3072]{0:T(1024)S(1)} %bitcast.210, bf16[3072,768]{1,0:T(8,128)(2,1)} %all-gather.22.cloned.1.call-done, bf16[4,256,768]{2,1,0:T(8,128)(2,1)S(1)} %copy-done.27, f32[4,768]{1,0:T(4,128)S(1)} %copy-done.36), kind=kOutput, calls=%fused_computation.174 | convolution fusion | flops 4903400448 | bytes 25196544 | tf_op jit(solution)/shard_map/scd,fd->scf/dot_general | solution.py:164
  287.4 10.2 multiply_reduce_fusion.2
  297.6 15.1 %fusion.67 = (f32[4,768]{1,0:T(4,128)}, bf16[4,256,768]{2,1,0:T(8,128)(2,1)}, f32[4,768]{1,0:T(4,128)}, f32[4,256,768]{2,1,0:T(8,128)S(1)}) fusion(bf16[4,256,768]{2,1,0:T(8,128)(2,1)S(1)} %copy-done.27, f32[768]{0:T(1024)S(1)} %copy-done.65, f32[4,256,768]{2,1,0:T(8,128)S(1)} %copy-done.18, f32[4,768]{1,0:T(4,128)S(1)} %copy-done.36, ...), kind=kOutput, calls=%fused_computation.96 | convolution fusion | flops 4877445120 | bytes 33114112 | tf_op jit(solution)/shard_map/scf,fd->scd/dot_general | solution.py:153
  317.4 178.6 %while.29 = (s32[]{:T(128)}, f32[2,2,256,12,64]{2,4,3,1,0:T(8,128)}, bf16[2,2,1024,768]{2,3,1,0:T(8,128)(2,1)}, bf16[2,2,1024,768]{2,3,1,0:T(8,128)(2,1)}, bf16[...) while((s32[]{:T(128)}, ...), condition=%wide.region_12.13_spmd.clone, body=%wide.region_10.12_spmd.sunk.clone | while | flops 4105562112 | bytes 316326176 | solution.py:223
  323.3 11.5 fusion.153
  334.8 12.2 %fusion.154 = bf16[2,12,64,1024]{3,2,1,0:T(8,128)(2,1)} fusion(f32[2,12,256,1024]{3,2,1,0:T(8,128)} %fusion.153, f32[2,12,256]{2,1,0:T(8,128)S(1)} %dynamic-slice_bitcast_fusion.3, bf16[2,2,256,12,64]{2,4,3,1,0:T(8,128)(2,1)S(1)} %copy-done.6, s32[]{:T(128)S(6)} %copy.135), kind=kOutput, calls=%fused_computation.18.clone.1.clone | convolution fusion | flops 824180736 | bytes 29130756 | tf_op jit(solution)/shard_map/while/body/eval_jaxpr/ghqk,gqhd->gkhd/dot_general | solution.py:200
  347.0 17.6 %multiply_reduce_fusion.12 = (f32[2,12,256]{2,1,0:T(8,128)S(1)}, f32[2,12,256,1024]{3,2,1,0:T(8,128)}) fusion(f32[2,12,256,1024]{3,2,1,0:T(8,128)} %fusion.153, f32[2,12,256]{2,1,0:T(8,128)S(1)} %dynamic-slice_bitcast_fusion.3, bf16[2,1024,12,64]{1,3,2,0:T(8,128)(2,1)} %bitcast.188, bf16[2,2,256,12,64]{2,4,3,1,0:T(8,128)(2,1)} %get-tuple-element.461, ...), kind=kOutput, calls=%fused_computation.15.clone.1.clone | convolution fusion | flops 830466048 | bytes 54312964 | tf_op jit(solution)/shard_map/while/body/eval_jaxpr/gqhd,gkhd->ghqk/dot_general | solution.py:203
  364.6 21.7 %multiply_convert_fusion.9 = bf16[2,12,256,1024]{3,2,1,0:T(8,128)(2,1)} fusion(f32[2,12,256,1024]{3,2,1,0:T(8,128)} %get-tuple-element.404, f32[2,12,256,1024]{3,2,1,0:T(8,128)} %fusion.153, f32[2,12,256]{2,1,0:T(8,128)S(1)} %get-tuple-element.405, f32[2,12,256]{2,1,0:T(8,128)S(1)} %dynamic-slice_bitcast_fusion.3), kind=kLoop, calls=%fused_computation.14.clone.1.clone | loop fusion | flops 31457280 | bytes 62963712 | tf_op jit(solution)/shard_map/while/body/eval_jaxpr/convert_element_type | solution.py:207
  412.4 11.5 fusion.153
  423.9 12.2 %fusion.154 = bf16[2,12,64,1024]{3,2,1,0:T(8,128)(2,1)} fusion(f32[2,12,256,1024]{3,2,1,0:T(8,128)} %fusion.153, f32[2,12,256]{2,1,0:T(8,128)S(1)} %dynamic-slice_bitcast_fusion.3, bf16[2,2,256,12,64]{2,4,3,1,0:T(8,128)(2,1)S(1)} %copy-done.6, s32[]{:T(128)S(6)} %copy.135), kind=kOutput, calls=%fused_computation.18.clone.1.clone | convolution fusion | flops 824180736 | bytes 29130756 | tf_op jit(solution)/shard_map/while/body/eval_jaxpr/ghqk,gqhd->gkhd/dot_general | solution.py:200
  436.1 17.6 %multiply_reduce_fusion.12 = (f32[2,12,256]{2,1,0:T(8,128)S(1)}, f32[2,12,256,1024]{3,2,1,0:T(8,128)}) fusion(f32[2,12,256,1024]{3,2,1,0:T(8,128)} %fusion.153, f32[2,12,256]{2,1,0:T(8,128)S(1)} %dynamic-slice_bitcast_fusion.3, bf16[2,1024,12,64]{1,3,2,0:T(8,128)(2,1)} %bitcast.188, bf16[2,2,256,12,64]{2,4,3,1,0:T(8,128)(2,1)} %get-tuple-element.461, ...), kind=kOutput, calls=%fused_computation.15.clone.1.clone | convolution fusion | flops 830466048 | bytes 54312964 | tf_op jit(solution)/shard_map/while/body/eval_jaxpr/gqhd,gkhd->ghqk/dot_general | solution.py:203
  453.7 21.7 %multiply_convert_fusion.9 = bf16[2,12,256,1024]{3,2,1,0:T(8,128)(2,1)} fusion(f32[2,12,256,1024]{3,2,1,0:T(8,128)} %get-tuple-element.404, f32[2,12,256,1024]{3,2,1,0:T(8,128)} %fusion.153, f32[2,12,256]{2,1,0:T(8,128)S(1)} %get-tuple-element.405, f32[2,12,256]{2,1,0:T(8,128)S(1)} %dynamic-slice_bitcast_fusion.3), kind=kLoop, calls=%fused_computation.14.clone.1.clone | loop fusion | flops 31457280 | bytes 62963712 | tf_op jit(solution)/shard_map/while/body/eval_jaxpr/convert_element_type | solution.py:207
  520.0 12.4 %bitcast_convert_fusion = bf16[3072,768]{1,0:T(8,128)(2,1)} fusion(bf16[4,256,768]{2,1,0:T(8,128)(2,1)S(1)} %copy-done.28, f32[4,768]{1,0:T(4,128)S(1)} %copy-done.37, f32[4,256,3072]{2,1,0:T(8,128)} %fusion.40, f32[3072]{0:T(1024)S(1)} %bitcast.212), kind=kOutput, calls=%fused_computation.53 | convolution fusion | flops 4868014080 | bytes 18898944 | tf_op jit(solution)/shard_map/scf,scd->fd/dot_general | solution.py:160
  534.4 10.0 bitcast_convert_fusion.1
  548.7 14.7 %reduce-scatter.9.cloned.1.call-done = bf16[4,256,768]{2,1,0:T(8,128)(2,1)} async-done(((bf16[4,1024,768]{2,1,0:T(8,128)(2,1)}), bf16[4,256,768]{2,1,0:T(8,128)(2,1)}) %reduce-scatter.9.cloned.1.call-update) | async-done | bytes 1572880 | tf_op jit(solution)/shard_map/reduce_scatter | solution.py:234
  589.9 34.6 %reduce-scatter.11.cloned.1.call-done = bf16[4,256,768]{2,1,0:T(8,128)(2,1)} async-done(((bf16[4,1024,768]{2,1,0:T(8,128)(2,1)}), bf16[4,256,768]{2,1,0:T(8,128)(2,1)}) %reduce-scatter.11.cloned.1.call-update) | async-done | bytes 1572880 | tf_op jit(solution)/shard_map/reduce_scatter | solution.py:240
  653.3 50.5 %reduce-scatter.19.cloned.1.call-done = bf16[768,768]{1,0:T(8,128)(2,1)} async-done(((bf16[3072,768]{1,0:T(8,128)(2,1)}), bf16[768,768]{1,0:T(8,128)(2,1)}) %reduce-scatter.19.cloned.1.call-update) | async-done | bytes 1179664 | tf_op jit(solution)/shard_map/reduce_scatter | solution.py:300
  703.8 50.3 %reduce-scatter.17.cloned.1.call-done = bf16[192,3072]{1,0:T(8,128)(2,1)} async-done(((bf16[768,3072]{1,0:T(8,128)(2,1)}), bf16[192,3072]{1,0:T(8,128)(2,1)}) %reduce-scatter.17.cloned.1.call-update) | async-done | bytes 1179664 | tf_op jit(solution)/shard_map/reduce_scatter | solution.py:294
  754.2 10.3 all-reduce.9
  777.4 28.7 %reduce-scatter.21.cloned.1.call-done = bf16[1152,128]{1,0:T(8,128)(2,1)} async-done(((bf16[4608,128]{1,0:T(8,128)(2,1)}), bf16[1152,128]{1,0:T(8,128)(2,1)}) %reduce-scatter.21.cloned.1.call-update) | async-done | bytes 294928 | tf_op jit(solution)/shard_map/reduce_scatter | solution.py:306
  806.1 43.0 %reduce-scatter.13.cloned.1.call-done = bf16[192,2304]{1,0:T(8,128)(2,1)} async-done(((bf16[768,2304]{1,0:T(8,128)(2,1)}), bf16[192,2304]{1,0:T(8,128)(2,1)}) %reduce-scatter.13.cloned.1.call-update) | async-done | bytes 884752 | tf_op jit(solution)/shard_map/reduce_scatter | solution.py:288
  849.1 306.4 %all-reduce.12 = (f32[192,2304]{1,0:T(8,128)}, f32[192,768]{1,0:T(8,128)}, f32[192,3072]{1,0:T(8,128)}, f32[768]{0:T(1024)}, f32[768,768]{1,0:T(8,128)}, /*index...) all-reduce(bf16[192,2304]{1,0:T(8,128)(2,1)} %reduce-scatter.13.clo, ...), channel_id=1, replica_groups=mesh['dp'=8,'seq'=4] {'dp'}, use_global_device_ids=true, to_apply=%region_18.19 | all-reduce | flops 1952192 | bytes 11718144 | tf_op jit(solution)/shard_map/psum | solution.py:322
  (308 shorter events, 269.1 us)
Async XLA Ops:
  7.2 23.1 %all-gather.10.cloned.1.call-start = ((), (), s32[]{:S(2)}) async-start(), calls=%async_computation.8 | async-start | bytes 1474560 | tf_op jit(solution)/shard_map/all_gather | solution.py:78
  8.0 54.3 %all-gather.12.cloned.1.call-start = ((), (), s32[]{:S(2)}) async-start(), calls=%async_computation.9 | async-start | bytes 4423680 | tf_op jit(solution)/shard_map/all_gather | solution.py:72
  8.7 113.2 %all-gather.14.cloned.1.call-start = ((), (), s32[]{:S(2)}) async-start(), calls=%async_computation.10 | async-start | bytes 7864320 | tf_op jit(solution)/shard_map/all_gather | solution.py:117
  21.7 46.7 %copy-start.42 = (f32[768]{0:T(1024)}, f32[768]{0:T(1024)S(1)}, u32[]{:S(2)}) copy-start(f32[768]{0:T(1024)S(1)} %convert_element_type.165) | copy-start | bytes 9220
  29.4 39.0 %copy-start.40 = (f32[4,256]{1,0:T(4,128)}, f32[4,256]{1,0:T(4,128)S(1)}, u32[]{:S(2)}) copy-start(f32[4,256]{1,0:T(4,128)S(1)} %broadcast_multiply_fusion.9) | copy-start | bytes 12292
  30.1 38.4 %copy-start.44 = (f32[4,256]{1,0:T(4,128)}, f32[4,256]{1,0:T(4,128)S(1)}, u32[]{:S(2)}) copy-start(f32[4,256]{1,0:T(4,128)S(1)} %add_rsqrt_fusion.1) | copy-start | bytes 12292
  33.2 35.3 %copy-start.48 = (f32[4,768]{1,0:T(4,128)}, f32[4,768]{1,0:T(4,128)S(1)}, u32[]{:S(2)}) copy-start(f32[4,768]{1,0:T(4,128)S(1)} %get-tuple-element.256) | copy-start | bytes 36868
  73.5 95.0 %all-gather.16.cloned.1.call-start = ((), (), s32[]{:S(2)}) async-start(), calls=%async_computation.11 | async-start | bytes 7864320 | tf_op jit(solution)/shard_map/all_gather | solution.py:116
  102.7 149.5 %all-gather.18.cloned.1.call-start = ((), (), s32[]{:S(2)}) async-start(), calls=%async_computation.12 | async-start | bytes 1474560 | tf_op jit(solution)/shard_map/all_gather | solution.py:73
  103.3 156.1 %all-gather.20.cloned.1.call-start = ((), (), s32[]{:S(2)}) async-start(), calls=%async_computation.13 | async-start | bytes 5898240 | tf_op jit(solution)/shard_map/all_gather | solution.py:74
  103.8 166.9 %all-gather.22.cloned.1.call-start = ((), (), s32[]{:S(2)}) async-start(), calls=%async_computation.14 | async-start | bytes 5898240 | tf_op jit(solution)/shard_map/all_gather | solution.py:76
  104.6 458.9 %reduce-scatter.9.cloned.1.call-start = ((), (), s32[]{:S(2)}) async-start(), calls=%async_computation.15 | async-start | bytes 7864320 | tf_op jit(solution)/shard_map/reduce_scatter | solution.py:234
  177.2 75.0 %copy-start.11 = (bf16[4,256,768]{2,1,0:T(8,128)(2,1)S(1)}, bf16[4,256,768]{2,1,0:T(8,128)(2,1)}, u32[]{:S(2)}) copy-start(bf16[4,256,768]{2,1,0:T(8,128)(2,1)} %param.19) | copy-start | bytes 4718596
  177.2 75.0 %copy-start.38 = (f32[4,768]{1,0:T(4,128)S(1)}, f32[4,768]{1,0:T(4,128)}, u32[]{:S(2)}) copy-start(f32[4,768]{1,0:T(4,128)} %get-tuple-element.258) | copy-start | bytes 36868
  257.3 40.3 %copy-start.46 = (f32[4,256]{1,0:T(4,128)}, f32[4,256]{1,0:T(4,128)S(1)}, u32[]{:S(2)}) copy-start(f32[4,256]{1,0:T(4,128)S(1)} %broadcast_multiply_fusion.8) | copy-start | bytes 12292
  259.4 38.2 %copy-start.67 = (f32[4,256]{1,0:T(4,128)}, f32[4,256]{1,0:T(4,128)S(1)}, u32[]{:S(2)}) copy-start(f32[4,256]{1,0:T(4,128)S(1)} %add_rsqrt_fusion) | copy-start | bytes 12292
  504.6 119.9 %reduce-scatter.11.cloned.1.call-start = ((), (), s32[]{:S(2)}) async-start(), calls=%async_computation.16 | async-start | bytes 7864320 | tf_op jit(solution)/shard_map/reduce_scatter | solution.py:240
  513.4 139.9 %reduce-scatter.15.cloned.1.call-start = ((), (), s32[]{:S(2)}) async-start(), calls=%async_computation.18 | async-start | bytes 1474560 | tf_op jit(solution)/shard_map/reduce_scatter | solution.py:291
  519.9 183.9 %reduce-scatter.19.cloned.1.call-start = ((), (), s32[]{:S(2)}) async-start(), calls=%async_computation.20 | async-start | bytes 5898240 | tf_op jit(solution)/shard_map/reduce_scatter | solution.py:300
  532.5 221.6 %reduce-scatter.17.cloned.1.call-start = ((), (), s32[]{:S(2)}) async-start(), calls=%async_computation.19 | async-start | bytes 5898240 | tf_op jit(solution)/shard_map/reduce_scatter | solution.py:294
  544.4 233.0 %reduce-scatter.23.cloned.1.call-start = ((), (), s32[]{:S(2)}) async-start(), calls=%async_computation.22 | async-start | bytes 327680 | tf_op jit(solution)/shard_map/reduce_scatter | solution.py:318
  582.9 41.6 %copy-start.35 = (f32[4,768]{1,0:T(4,128)S(1)}, f32[4,768]{1,0:T(4,128)}, u32[]{:S(2)}) copy-start(f32[4,768]{1,0:T(4,128)} %copy-done.34) | copy-start | bytes 36868
  582.9 41.6 %copy-start.41 = (f32[4,256]{1,0:T(4,128)S(1)}, f32[4,256]{1,0:T(4,128)}, u32[]{:S(2)}) copy-start(f32[4,256]{1,0:T(4,128)} %copy-done.40) | copy-start | bytes 12292
  582.9 41.6 %copy-start.43 = (f32[768]{0:T(1024)S(1)}, f32[768]{0:T(1024)}, u32[]{:S(2)}) copy-start(f32[768]{0:T(1024)} %copy-done.42) | copy-start | bytes 9220
  582.9 41.6 %copy-start.45 = (f32[4,256]{1,0:T(4,128)S(1)}, f32[4,256]{1,0:T(4,128)}, u32[]{:S(2)}) copy-start(f32[4,256]{1,0:T(4,128)} %copy-done.44) | copy-start | bytes 12292
  635.9 170.2 %reduce-scatter.21.cloned.1.call-start = ((), (), s32[]{:S(2)}) async-start(), calls=%async_computation.21 | async-start | bytes 1474560 | tf_op jit(solution)/shard_map/reduce_scatter | solution.py:306
  640.8 208.3 %reduce-scatter.13.cloned.1.call-start = ((), (), s32[]{:S(2)}) async-start(), calls=%async_computation.17 | async-start | bytes 4423680 | tf_op jit(solution)/shard_map/reduce_scatter | solution.py:288
  649.0 105.1 %copy-start.62 = (bf16[3072]{0:T(1024)(128)(2,1)S(1)}, bf16[3072]{0:T(1024)(128)(2,1)}, u32[]{:S(2)}) copy-start(bf16[3072]{0:T(1024)(128)(2,1)} %get-tuple-element.264) | copy-start | bytes 18436
  649.0 105.1 %copy-start.70 = (bf16[768]{0:T(1024)(128)(2,1)S(1)}, bf16[768]{0:T(1024)(128)(2,1)}, u32[]{:S(2)}) copy-start(bf16[768]{0:T(1024)(128)(2,1)} %get-tuple-element.160) | copy-start | bytes 4612
  764.8 84.3 %copy-start.30 = (bf16[768,768]{1,0:T(8,128)(2,1)S(1)}, bf16[768,768]{1,0:T(8,128)(2,1)}, u32[]{:S(2)}) copy-start(bf16[768,768]{1,0:T(8,128)(2,1)} %reduce-scatter.19.cloned.1.call-done) | copy-start | bytes 3538948
  764.8 84.3 %copy-start.33 = (bf16[192,768]{1,0:T(8,128)(2,1)S(1)}, bf16[192,768]{1,0:T(8,128)(2,1)}, u32[]{:S(2)}) copy-start(bf16[192,768]{1,0:T(8,128)(2,1)} %reduce-scatter.15.cloned.1.call-done) | copy-start | bytes 884740
  764.8 390.7 %copy-start.1 = (bf16[1024,128]{1,0:T(8,128)(2,1)S(1)}, bf16[1024,128]{1,0:T(8,128)(2,1)}, u32[]{:S(2)}) copy-start(bf16[1024,128]{1,0:T(8,128)(2,1)} %param.20) | copy-start | bytes 786436
  (64 other events, 538.6 us)
Sparse Core Ops, SparseCore 0:
  9.6 20.2 all-gather.9
  31.5 30.7 all-gather.11
  73.6 46.4 all-gather.13
  122.1 46.3 all-gather.15
  169.9 17.4 all-gather.17
  188.8 37.4 all-gather.19
  227.9 37.4 all-gather.21
  504.8 58.6 reduce-scatter.8
  566.1 58.3 reduce-scatter.10
  627.5 25.7 reduce-scatter.14
  656.0 47.8 reduce-scatter.18
  706.2 47.8 reduce-scatter.16
  757.3 20.0 reduce-scatter.22
  780.3 25.7 reduce-scatter.20
  808.7 40.4 reduce-scatter.12
where the time goes:
time: 1170 us; the launch traced here: 1160 us
  blocking collectives  336 us (29%)
  waiting for transfers between devices  302 us (26%)
  matrix products  279 us (24%)
  local copies, waits for them, and re-layouts  113 us (10%)
  other arithmetic  113 us (10%)
  between operations  17.8 us (2%)
    psum x1, blocking collectives, shards(): lax.psum((shares[0], shares[1], shares[2], shares[3], shares[4], shares[5...  306 us
    reduce_scatter x1, waiting for transfers between devices, shards(): lax.psum_scatter(terms[4].astype(jnp.bfloat16), 'seq', scatter_dimension=...  50.5 us
    reduce_scatter x1, waiting for transfers between devices, shards(): lax.psum_scatter(terms[2].astype(jnp.bfloat16), 'seq', scatter_dimension=...  50.3 us
    convert_element_type x2, other arithmetic, attend_back(): scores_grad = (probs * (probs_grad - center)).astype(low_type)  43.4 us
    reduce_scatter x1, waiting for transfers between devices, shards(): lax.psum_scatter(terms[0].astype(jnp.bfloat16), 'seq', scatter_dimension=...  43 us
    all_gather x1, waiting for transfers between devices, shards(): lax.all_gather(keys_local, 'seq', axis=1, tiled=True)  37.9 us
    dot_general x2, matrix products, attend_back(): jnp.einsum('gqhd,gkhd->ghqk', mixed_grad_b, values_h, preferred_element_t...  35.2 us
    reduce_scatter x1, waiting for transfers between devices, shards(): lax.psum_scatter(values_term.reshape(seqs, length, width).astype(jnp.bflo...  34.6 us
  transfers between devices with their start and end apart: 15, of which 10 were waited for; matrix products, arithmetic and copies ran while one was open for 22% of the time, Pallas kernels for 0%

commit v1 on v0

--- a/solution.py
+++ b/solution.py
@@ -7,6 +7,18 @@
 
 HEADS = 12
 EPSILON = 1e-05
+
+
+def gather_by_bits(shard, axis, dim):
+    ways, here, step = (lax.axis_size(axis), lax.axis_index(axis), shard.shape[dim])
+    line, have = (shard, 1)
+    while have < ways:
+        line = jnp.concatenate(
+            [line, lax.ppermute(line, axis, [(d, (d - have) % ways) for d in range(ways)])],
+            axis=dim,
+        )
+        have = 2 * have
+    return jnp.roll(line, here * step, axis=dim)
 
 
 def rotate_half(values):
@@ -69,7 +81,7 @@
     head_width = width // HEADS
     scale = 1.0 / math.sqrt(head_width)
     gathered = (
-        lax.all_gather(heads_weight, "seq", axis=0, tiled=True),
+        gather_by_bits(heads_weight, "seq", 0),
         lax.all_gather(merge_weight, "seq", axis=0, tiled=True),
         lax.all_gather(lift_weight, "seq", axis=0, tiled=True),
         lax.all_gather(lift_bias, "seq", axis=0, tiled=True),

time: 1170 us -> 1190 us (1.017)
    ppermute x0 -> x2, waiting for transfers between devices: none -> 36.4 us  [gather_by_bits(): lax.ppermute(line, axis, [(d, (d - have) % ways) for d in range(ways)])]
    all_gather x1 -> x0, waiting for transfers between devices: 29.1 us -> none  [shards(): lax.all_gather(heads_weight, 'seq', axis=0, tiled=True)]
  transfers between devices with their start and end apart: 15 -> 16, of which waited for: 10 -> 10; matrix products, arithmetic and copies ran while one was open for 22% -> 21% of each run, Pallas kernels for 0% -> 0%
where the time goes in v1:
time: 1190 us; the launch traced here: 1180 us
  blocking collectives  338 us (28%)
  waiting for transfers between devices  309 us (26%)
  matrix products  279 us (23%)
  local copies, waits for them, and re-layouts  119 us (10%)
  other arithmetic  115 us (10%)
  between operations  18 us (2%)
    psum x1, blocking collectives, shards(): lax.psum((shares[0], shares[1], shares[2], shares[3], shares[4], shares[5...  306 us
    reduce_scatter x1, waiting for transfers between devices, shards(): lax.psum_scatter(terms[2].astype(jnp.bfloat16), 'seq', scatter_dimension=...  50.5 us
    reduce_scatter x1, waiting for transfers between devices, shards(): lax.psum_scatter(terms[4].astype(jnp.bfloat16), 'seq', scatter_dimension=...  50.4 us
    convert_element_type x2, other arithmetic, attend_back(): scores_grad = (probs * (probs_grad - center)).astype(low_type)  43.4 us
    reduce_scatter x1, waiting for transfers between devices, shards(): lax.psum_scatter(terms[0].astype(jnp.bfloat16), 'seq', scatter_dimension=...  43 us
    all_gather x1, waiting for transfers between devices, shards(): lax.all_gather(keys_local, 'seq', axis=1, tiled=True)  38.4 us
    ppermute x2, waiting for transfers between devices, gather_by_bits(): lax.ppermute(line, axis, [(d, (d - have) % ways) for d in range(ways)])  36.4 us
    dot_general x2, matrix products, attend_back(): jnp.einsum('gqhd,gkhd->ghqk', mixed_grad_b, values_h, preferred_element_t...  35.2 us
  transfers between devices with their start and end apart: 16, of which 10 were waited for; matrix products, arithmetic and copies ran while one was open for 21% of the time, Pallas kernels for 0%

profile of v1, /device:TPU:0, one launch (start us, length us, event | category | flops | bytes accessed | tf_op | source)
XLA Modules:
  0.0 1182.5 jit_solution(12861678087886881850)
XLA Ops:
  15.5 10.5 all-reduce.10
  37.3 36.4 %collective-permute-done.1 = bf16[384,2304]{1,0:T(8,128)(2,1)} collective-permute-done((bf16[384,2304]{1,0:T(8,128)(2,1)}, bf16[384,2304]{1,0:T(8,128)(2,1)}, u32[]{:S(2)}, u32[]{:S(2)}) %collective-permute-start.1) | collective-permute-done | bytes 1769504 | tf_op jit(solution)/shard_map/ppermute | solution.py:17
  150.0 38.4 %all-gather.13.cloned.1.call-done = bf16[4,1024,768]{2,1,0:T(8,128)(2,1)} async-done(((bf16[4,256,768]{2,1,0:T(8,128)(2,1)}), bf16[4,1024,768]{2,1,0:T(8,128)(2,1)}) %all-gather.13.cloned.1.call-update) | async-done | bytes 6291472 | tf_op jit(solution)/shard_map/all_gather | solution.py:128
  197.2 74.9 %while.28 = (s32[]{:T(128)}, bf16[2,2,256,12,64]{2,4,3,1,0:T(8,128)(2,1)}, f32[2,2,12,256]{3,2,1,0:T(8,128)S(1)}, bf16[2,2,1024,768]{2,3,1,0:T(8,128)(2,1)}, bf1...) while((s32[]{:T(128)}, bf16[2,2,256,12,64]{2,4,3,1,0:T(8,128)(2,1)}, ...), condition=%wide.region_5.6_spmd.clone, body=%wide.region_2.5_spmd.sunk.clone | while | flops 1667229696 | bytes 96952408 | solution.py:152
  200.8 10.2 multiply_reduce_fusion.11
  211.1 11.6 fusion.147
  222.7 11.8 bitcast_dynamic-update-slice_fusion.9
  238.2 10.3 multiply_reduce_fusion.11
  248.5 11.8 fusion.147
  260.3 11.8 bitcast_dynamic-update-slice_fusion.9
  279.4 11.3 fusion.40
  290.7 16.6 %fusion.97 = (bf16[3072]{0:T(1024)(128)(2,1)}, bf16[4,256,3072]{2,1,0:T(8,128)(2,1)}) fusion(f32[4,256,3072]{2,1,0:T(8,128)} %fusion.40, f32[3072]{0:T(1024)S(1)} %bitcast.210, bf16[3072,768]{1,0:T(8,128)(2,1)} %all-gather.19.cloned.1.call-done, bf16[4,256,768]{2,1,0:T(8,128)(2,1)S(1)} %copy-done.28, f32[4,768]{1,0:T(4,128)S(1)} %copy-done.37), kind=kOutput, calls=%fused_computation.185 | convolution fusion | flops 4903400448 | bytes 25196544 | tf_op jit(solution)/shard_map/scd,fd->scf/dot_general | solution.py:176
  307.3 10.2 multiply_reduce_fusion.2
  317.5 15.1 %fusion.67 = (f32[4,768]{1,0:T(4,128)}, bf16[4,256,768]{2,1,0:T(8,128)(2,1)}, f32[4,768]{1,0:T(4,128)}, f32[4,256,768]{2,1,0:T(8,128)S(1)}) fusion(bf16[4,256,768]{2,1,0:T(8,128)(2,1)S(1)} %copy-done.28, f32[768]{0:T(1024)S(1)} %copy-done.66, f32[4,256,768]{2,1,0:T(8,128)S(1)} %copy-done.18, f32[4,768]{1,0:T(4,128)S(1)} %copy-done.37, ...), kind=kOutput, calls=%fused_computation.96 | convolution fusion | flops 4877445120 | bytes 33114112 | tf_op jit(solution)/shard_map/scf,fd->scd/dot_general | solution.py:165
  337.3 178.3 %while.29 = (s32[]{:T(128)}, f32[2,2,256,12,64]{2,4,3,1,0:T(8,128)}, bf16[2,2,1024,768]{2,3,1,0:T(8,128)(2,1)}, bf16[2,2,1024,768]{2,3,1,0:T(8,128)(2,1)}, bf16[...) while((s32[]{:T(128)}, ...), condition=%wide.region_12.13_spmd.clone, body=%wide.region_10.12_spmd.sunk.clone | while | flops 4105562112 | bytes 316326176 | solution.py:235
  343.5 11.4 fusion.157
  354.9 12.2 %fusion.158 = bf16[2,12,64,1024]{3,2,1,0:T(8,128)(2,1)} fusion(f32[2,12,256,1024]{3,2,1,0:T(8,128)} %fusion.157, f32[2,12,256]{2,1,0:T(8,128)S(1)} %dynamic-slice_bitcast_fusion.3, bf16[2,2,256,12,64]{2,4,3,1,0:T(8,128)(2,1)S(1)} %copy-done.6, s32[]{:T(128)S(6)} %copy.140), kind=kOutput, calls=%fused_computation.18.clone.1.clone | convolution fusion | flops 824180736 | bytes 29130756 | tf_op jit(solution)/shard_map/while/body/eval_jaxpr/ghqk,gqhd->gkhd/dot_general | solution.py:212
  367.1 17.6 %multiply_reduce_fusion.12 = (f32[2,12,256]{2,1,0:T(8,128)S(1)}, f32[2,12,256,1024]{3,2,1,0:T(8,128)}) fusion(f32[2,12,256,1024]{3,2,1,0:T(8,128)} %fusion.157, f32[2,12,256]{2,1,0:T(8,128)S(1)} %dynamic-slice_bitcast_fusion.3, bf16[2,1024,12,64]{1,3,2,0:T(8,128)(2,1)} %bitcast.188, bf16[2,2,256,12,64]{2,4,3,1,0:T(8,128)(2,1)} %get-tuple-element.461, ...), kind=kOutput, calls=%fused_computation.15.clone.1.clone | convolution fusion | flops 830466048 | bytes 54312964 | tf_op jit(solution)/shard_map/while/body/eval_jaxpr/gqhd,gkhd->ghqk/dot_general | solution.py:215
  384.7 21.7 %multiply_convert_fusion.9 = bf16[2,12,256,1024]{3,2,1,0:T(8,128)(2,1)} fusion(f32[2,12,256,1024]{3,2,1,0:T(8,128)} %get-tuple-element.404, f32[2,12,256,1024]{3,2,1,0:T(8,128)} %fusion.157, f32[2,12,256]{2,1,0:T(8,128)S(1)} %get-tuple-element.405, f32[2,12,256]{2,1,0:T(8,128)S(1)} %dynamic-slice_bitcast_fusion.3), kind=kLoop, calls=%fused_computation.14.clone.1.clone | loop fusion | flops 31457280 | bytes 62963712 | tf_op jit(solution)/shard_map/while/body/eval_jaxpr/convert_element_type | solution.py:219
  432.4 11.4 fusion.157
  443.8 12.2 %fusion.158 = bf16[2,12,64,1024]{3,2,1,0:T(8,128)(2,1)} fusion(f32[2,12,256,1024]{3,2,1,0:T(8,128)} %fusion.157, f32[2,12,256]{2,1,0:T(8,128)S(1)} %dynamic-slice_bitcast_fusion.3, bf16[2,2,256,12,64]{2,4,3,1,0:T(8,128)(2,1)S(1)} %copy-done.6, s32[]{:T(128)S(6)} %copy.140), kind=kOutput, calls=%fused_computation.18.clone.1.clone | convolution fusion | flops 824180736 | bytes 29130756 | tf_op jit(solution)/shard_map/while/body/eval_jaxpr/ghqk,gqhd->gkhd/dot_general | solution.py:212
  456.0 17.6 %multiply_reduce_fusion.12 = (f32[2,12,256]{2,1,0:T(8,128)S(1)}, f32[2,12,256,1024]{3,2,1,0:T(8,128)}) fusion(f32[2,12,256,1024]{3,2,1,0:T(8,128)} %fusion.157, f32[2,12,256]{2,1,0:T(8,128)S(1)} %dynamic-slice_bitcast_fusion.3, bf16[2,1024,12,64]{1,3,2,0:T(8,128)(2,1)} %bitcast.188, bf16[2,2,256,12,64]{2,4,3,1,0:T(8,128)(2,1)} %get-tuple-element.461, ...), kind=kOutput, calls=%fused_computation.15.clone.1.clone | convolution fusion | flops 830466048 | bytes 54312964 | tf_op jit(solution)/shard_map/while/body/eval_jaxpr/gqhd,gkhd->ghqk/dot_general | solution.py:215
  473.6 21.7 %multiply_convert_fusion.9 = bf16[2,12,256,1024]{3,2,1,0:T(8,128)(2,1)} fusion(f32[2,12,256,1024]{3,2,1,0:T(8,128)} %get-tuple-element.404, f32[2,12,256,1024]{3,2,1,0:T(8,128)} %fusion.157, f32[2,12,256]{2,1,0:T(8,128)S(1)} %get-tuple-element.405, f32[2,12,256]{2,1,0:T(8,128)S(1)} %dynamic-slice_bitcast_fusion.3), kind=kLoop, calls=%fused_computation.14.clone.1.clone | loop fusion | flops 31457280 | bytes 62963712 | tf_op jit(solution)/shard_map/while/body/eval_jaxpr/convert_element_type | solution.py:219
  539.7 12.5 %bitcast_convert_fusion = bf16[3072,768]{1,0:T(8,128)(2,1)} fusion(bf16[4,256,768]{2,1,0:T(8,128)(2,1)S(1)} %copy-done.29, f32[4,768]{1,0:T(4,128)S(1)} %copy-done.38, f32[4,256,3072]{2,1,0:T(8,128)} %fusion.40, f32[3072]{0:T(1024)S(1)} %bitcast.212), kind=kOutput, calls=%fused_computation.53 | convolution fusion | flops 4868014080 | bytes 18898944 | tf_op jit(solution)/shard_map/scf,scd->fd/dot_general | solution.py:172
  568.4 14.9 %reduce-scatter.9.cloned.1.call-done = bf16[4,256,768]{2,1,0:T(8,128)(2,1)} async-done(((bf16[4,1024,768]{2,1,0:T(8,128)(2,1)}), bf16[4,256,768]{2,1,0:T(8,128)(2,1)}) %reduce-scatter.9.cloned.1.call-update) | async-done | bytes 1572880 | tf_op jit(solution)/shard_map/reduce_scatter | solution.py:246
  609.7 34.7 %reduce-scatter.11.cloned.1.call-done = bf16[4,256,768]{2,1,0:T(8,128)(2,1)} async-done(((bf16[4,1024,768]{2,1,0:T(8,128)(2,1)}), bf16[4,256,768]{2,1,0:T(8,128)(2,1)}) %reduce-scatter.11.cloned.1.call-update) | async-done | bytes 1572880 | tf_op jit(solution)/shard_map/reduce_scatter | solution.py:252
  673.3 50.4 %reduce-scatter.19.cloned.1.call-done = bf16[768,768]{1,0:T(8,128)(2,1)} async-done(((bf16[3072,768]{1,0:T(8,128)(2,1)}), bf16[768,768]{1,0:T(8,128)(2,1)}) %reduce-scatter.19.cloned.1.call-update) | async-done | bytes 1179664 | tf_op jit(solution)/shard_map/reduce_scatter | solution.py:312
  723.7 50.5 %reduce-scatter.17.cloned.1.call-done = bf16[192,3072]{1,0:T(8,128)(2,1)} async-done(((bf16[768,3072]{1,0:T(8,128)(2,1)}), bf16[192,3072]{1,0:T(8,128)(2,1)}) %reduce-scatter.17.cloned.1.call-update) | async-done | bytes 1179664 | tf_op jit(solution)/shard_map/reduce_scatter | solution.py:306
  774.2 10.3 all-reduce.9
  797.3 28.9 %reduce-scatter.21.cloned.1.call-done = bf16[1152,128]{1,0:T(8,128)(2,1)} async-done(((bf16[4608,128]{1,0:T(8,128)(2,1)}), bf16[1152,128]{1,0:T(8,128)(2,1)}) %reduce-scatter.21.cloned.1.call-update) | async-done | bytes 294928 | tf_op jit(solution)/shard_map/reduce_scatter | solution.py:318
  826.2 43.0 %reduce-scatter.13.cloned.1.call-done = bf16[192,2304]{1,0:T(8,128)(2,1)} async-done(((bf16[768,2304]{1,0:T(8,128)(2,1)}), bf16[192,2304]{1,0:T(8,128)(2,1)}) %reduce-scatter.13.cloned.1.call-update) | async-done | bytes 884752 | tf_op jit(solution)/shard_map/reduce_scatter | solution.py:300
  869.2 306.4 %all-reduce.12 = (f32[192,2304]{1,0:T(8,128)}, f32[192,768]{1,0:T(8,128)}, f32[192,3072]{1,0:T(8,128)}, f32[768]{0:T(1024)}, f32[768,768]{1,0:T(8,128)}, /*index...) all-reduce(bf16[192,2304]{1,0:T(8,128)(2,1)} %reduce-scatter.13.clo, ...), channel_id=1, replica_groups=mesh['dp'=8,'seq'=4] {'dp'}, use_global_device_ids=true, to_apply=%region_18.19 | all-reduce | flops 1952192 | bytes 11718144 | tf_op jit(solution)/shard_map/psum | solution.py:334
  (328 shorter events, 280.4 us)
Async XLA Ops:
  7.3 27.8 %all-gather.9.cloned.1.call-start = ((), (), s32[]{:S(2)}) async-start(), calls=%async_computation.8 | async-start | bytes 1474560 | tf_op jit(solution)/shard_map/all_gather | solution.py:90
  7.3 24.0 %collective-permute-start = (bf16[192,2304]{1,0:T(8,128)(2,1)}, bf16[192,2304]{1,0:T(8,128)(2,1)S(1)}, u32[]{:S(2)}, u32[]{:S(2)}) collective-permute-start(bf16[192,2304]{1,0:T(8,128)(2,1)} %param.23), channel_id=1, source_target_pairs={{0,3},{1,0},{2,1},{3,2},{4,7},{5,4},{6,5},{7,6},{8,11},{9,8},{10,9... | collective-permute-start | bytes 2654216 | tf_op jit(solution)/shard_map/ppermute | solution.py:17
  9.8 131.5 %all-gather.11.cloned.1.call-start = ((), (), s32[]{:S(2)}) async-start(), calls=%async_computation.9 | async-start | bytes 7864320 | tf_op jit(solution)/shard_map/all_gather | solution.py:129
  11.5 70.0 %copy-start.41 = (f32[4,256]{1,0:T(4,128)}, f32[4,256]{1,0:T(4,128)S(1)}, u32[]{:S(2)}) copy-start(f32[4,256]{1,0:T(4,128)S(1)} %broadcast_multiply_fusion.9) | copy-start | bytes 12292
  26.1 55.4 %copy-start.43 = (f32[768]{0:T(1024)}, f32[768]{0:T(1024)S(1)}, u32[]{:S(2)}) copy-start(f32[768]{0:T(1024)S(1)} %convert_element_type.165) | copy-start | bytes 9220
  32.6 41.1 %collective-permute-start.1 = (bf16[384,2304]{1,0:T(8,128)(2,1)}, bf16[384,2304]{1,0:T(8,128)(2,1)}, u32[]{:S(2)}, u32[]{:S(2)}) collective-permute-start(bf16[384,2304]{1,0:T(8,128)(2,1)} %pad_maximum_fusion.5), channel_id=1, source_target_pairs={{0,2},{1,3},{2,0},{3,1},{4,6},{5,7},{6,4},{7,5},{8,10},{9,11},{10,... | collective-permute-start | bytes 5308424 | tf_op jit(solution)/shard_map/ppermute | solution.py:17
  32.8 48.6 %copy-start.45 = (f32[4,256]{1,0:T(4,128)}, f32[4,256]{1,0:T(4,128)S(1)}, u32[]{:S(2)}) copy-start(f32[4,256]{1,0:T(4,128)S(1)} %add_rsqrt_fusion.1) | copy-start | bytes 12292
  37.3 44.2 %copy-start.35 = (f32[4,768]{1,0:T(4,128)}, f32[4,768]{1,0:T(4,128)S(1)}, u32[]{:S(2)}) copy-start(f32[4,768]{1,0:T(4,128)S(1)} %get-tuple-element.257) | copy-start | bytes 36868
  37.3 44.2 %copy-start.49 = (f32[4,768]{1,0:T(4,128)}, f32[4,768]{1,0:T(4,128)S(1)}, u32[]{:S(2)}) copy-start(f32[4,768]{1,0:T(4,128)S(1)} %get-tuple-element.256) | copy-start | bytes 36868
  92.8 95.7 %all-gather.13.cloned.1.call-start = ((), (), s32[]{:S(2)}) async-start(), calls=%async_computation.10 | async-start | bytes 7864320 | tf_op jit(solution)/shard_map/all_gather | solution.py:128
  122.0 150.1 %all-gather.15.cloned.1.call-start = ((), (), s32[]{:S(2)}) async-start(), calls=%async_computation.11 | async-start | bytes 1474560 | tf_op jit(solution)/shard_map/all_gather | solution.py:85
  122.6 156.7 %all-gather.17.cloned.1.call-start = ((), (), s32[]{:S(2)}) async-start(), calls=%async_computation.12 | async-start | bytes 5898240 | tf_op jit(solution)/shard_map/all_gather | solution.py:86
  123.2 167.5 %all-gather.19.cloned.1.call-start = ((), (), s32[]{:S(2)}) async-start(), calls=%async_computation.13 | async-start | bytes 5898240 | tf_op jit(solution)/shard_map/all_gather | solution.py:88
  123.8 459.5 %reduce-scatter.9.cloned.1.call-start = ((), (), s32[]{:S(2)}) async-start(), calls=%async_computation.14 | async-start | bytes 7864320 | tf_op jit(solution)/shard_map/reduce_scatter | solution.py:246
  197.2 74.9 %copy-start.11 = (bf16[4,256,768]{2,1,0:T(8,128)(2,1)S(1)}, bf16[4,256,768]{2,1,0:T(8,128)(2,1)}, u32[]{:S(2)}) copy-start(bf16[4,256,768]{2,1,0:T(8,128)(2,1)} %param.19) | copy-start | bytes 4718596
  197.2 74.9 %copy-start.39 = (f32[4,768]{1,0:T(4,128)S(1)}, f32[4,768]{1,0:T(4,128)}, u32[]{:S(2)}) copy-start(f32[4,768]{1,0:T(4,128)} %get-tuple-element.258) | copy-start | bytes 36868
  524.3 120.1 %reduce-scatter.11.cloned.1.call-start = ((), (), s32[]{:S(2)}) async-start(), calls=%async_computation.15 | async-start | bytes 7864320 | tf_op jit(solution)/shard_map/reduce_scatter | solution.py:252
  533.2 140.1 %reduce-scatter.15.cloned.1.call-start = ((), (), s32[]{:S(2)}) async-start(), calls=%async_computation.17 | async-start | bytes 1474560 | tf_op jit(solution)/shard_map/reduce_scatter | solution.py:303
  539.7 184.0 %reduce-scatter.19.cloned.1.call-start = ((), (), s32[]{:S(2)}) async-start(), calls=%async_computation.19 | async-start | bytes 5898240 | tf_op jit(solution)/shard_map/reduce_scatter | solution.py:312
  552.3 221.9 %reduce-scatter.17.cloned.1.call-start = ((), (), s32[]{:S(2)}) async-start(), calls=%async_computation.18 | async-start | bytes 5898240 | tf_op jit(solution)/shard_map/reduce_scatter | solution.py:306
  564.1 233.2 %reduce-scatter.23.cloned.1.call-start = ((), (), s32[]{:S(2)}) async-start(), calls=%async_computation.21 | async-start | bytes 327680 | tf_op jit(solution)/shard_map/reduce_scatter | solution.py:330
  602.7 41.7 %copy-start.36 = (f32[4,768]{1,0:T(4,128)S(1)}, f32[4,768]{1,0:T(4,128)}, u32[]{:S(2)}) copy-start(f32[4,768]{1,0:T(4,128)} %copy-done.35) | copy-start | bytes 36868
  602.7 41.7 %copy-start.42 = (f32[4,256]{1,0:T(4,128)S(1)}, f32[4,256]{1,0:T(4,128)}, u32[]{:S(2)}) copy-start(f32[4,256]{1,0:T(4,128)} %copy-done.41) | copy-start | bytes 12292
  602.7 41.7 %copy-start.44 = (f32[768]{0:T(1024)S(1)}, f32[768]{0:T(1024)}, u32[]{:S(2)}) copy-start(f32[768]{0:T(1024)} %copy-done.43) | copy-start | bytes 9220
  602.8 41.6 %copy-start.46 = (f32[4,256]{1,0:T(4,128)S(1)}, f32[4,256]{1,0:T(4,128)}, u32[]{:S(2)}) copy-start(f32[4,256]{1,0:T(4,128)} %copy-done.45) | copy-start | bytes 12292
  656.0 170.1 %reduce-scatter.21.cloned.1.call-start = ((), (), s32[]{:S(2)}) async-start(), calls=%async_computation.20 | async-start | bytes 1474560 | tf_op jit(solution)/shard_map/reduce_scatter | solution.py:318
  661.2 208.0 %reduce-scatter.13.cloned.1.call-start = ((), (), s32[]{:S(2)}) async-start(), calls=%async_computation.16 | async-start | bytes 4423680 | tf_op jit(solution)/shard_map/reduce_scatter | solution.py:300
  669.1 105.1 %copy-start.63 = (bf16[3072]{0:T(1024)(128)(2,1)S(1)}, bf16[3072]{0:T(1024)(128)(2,1)}, u32[]{:S(2)}) copy-start(bf16[3072]{0:T(1024)(128)(2,1)} %get-tuple-element.264) | copy-start | bytes 18436
  669.1 105.1 %copy-start.73 = (bf16[768]{0:T(1024)(128)(2,1)S(1)}, bf16[768]{0:T(1024)(128)(2,1)}, u32[]{:S(2)}) copy-start(bf16[768]{0:T(1024)(128)(2,1)} %get-tuple-element.160) | copy-start | bytes 4612
  784.9 84.3 %copy-start.31 = (bf16[768,768]{1,0:T(8,128)(2,1)S(1)}, bf16[768,768]{1,0:T(8,128)(2,1)}, u32[]{:S(2)}) copy-start(bf16[768,768]{1,0:T(8,128)(2,1)} %reduce-scatter.19.cloned.1.call-done) | copy-start | bytes 3538948
  784.9 84.3 %copy-start.34 = (bf16[192,768]{1,0:T(8,128)(2,1)S(1)}, bf16[192,768]{1,0:T(8,128)(2,1)}, u32[]{:S(2)}) copy-start(bf16[192,768]{1,0:T(8,128)(2,1)} %reduce-scatter.15.cloned.1.call-done) | copy-start | bytes 884740
  784.9 390.7 %copy-start.1 = (bf16[1024,128]{1,0:T(8,128)(2,1)S(1)}, bf16[1024,128]{1,0:T(8,128)(2,1)}, u32[]{:S(2)}) copy-start(bf16[1024,128]{1,0:T(8,128)(2,1)} %param.20) | copy-start | bytes 786436
  (71 other events, 643.7 us)
Sparse Core Ops, SparseCore 0:
  9.9 20.0 all-gather.8
  92.9 46.9 all-gather.10
  142.1 46.3 all-gather.12
  189.9 17.4 all-gather.14
  208.8 37.4 all-gather.16
  247.7 37.4 all-gather.18
  524.4 58.7 reduce-scatter.8
  586.0 58.3 reduce-scatter.10
  647.5 25.7 reduce-scatter.14
  675.8 47.8 reduce-scatter.18
  726.2 47.8 reduce-scatter.16
  777.2 20.0 reduce-scatter.22
  800.4 25.6 reduce-scatter.20
  828.7 40.4 reduce-scatter.12
